TPU v7x, 32 devices: a whole 2x2x4 slice. The times are simulated.
32 devices in a mesh: row: 8 (over z, core), loop: 4 (over y, x).
Axes of the slice: x: 2, y: 2, z: 4, core: 2. Of those that a mesh axis runs over, the one named last changes fastest.
Arguments:
- student_image: bfloat16 [5120, 1024], P(('row', 'loop')), may hold values from -12 to 12
- student_text: bfloat16 [5120, 1024], P(('row', 'loop')), may hold values from -12 to 12
- teacher_image: bfloat16 [5120, 1024], P('row', 'loop'), may hold values from -12 to 12
- teacher_text: bfloat16 [5120, 1024], P('row', 'loop'), may hold values from -12 to 12
- student_scale: float32 [1], replicated, may hold values from 30 to 100
- teacher_scale: float32 [1], replicated, may hold values from 30 to 100
Outputs:
- loss: float32 [1], replicated
- grad_image: bfloat16 [5120, 1024], P(('row', 'loop'))
- grad_text: bfloat16 [5120, 1024], P(('row', 'loop'))
All inputs are finite; a program needn't handle non-finite values.
Results may differ from a plain program's by a relative error of at most 0.014.
The roundings to bfloat16 on the way count: a program that leaves them out, or rounds other values in their place, can miss the bound.
Values may be sent and summed in bfloat16 or wider, within the bound.
A program may use at most 128 MiB of HBM per device.

v0:
```python
import jax
import jax.numpy as jnp
from jax import lax
from jax.sharding import PartitionSpec as P

EPS = 1e-06


def unit_rows(codes):
    values = codes.astype(jnp.float32)
    norms = jnp.sqrt(jnp.sum(values * values, axis=1, keepdims=True) + EPS)
    return (values / norms, norms)


def back_norm(grad_unit, units, norms):
    inner = jnp.sum(grad_unit * units, axis=1, keepdims=True)
    return ((grad_unit - units * inner) / norms).astype(jnp.bfloat16)


def on_device(
    student_image, student_text, teacher_image, teacher_text, student_scale, teacher_scale
):
    simg_unit, simg_norm = unit_rows(student_image)
    stxt_unit, stxt_norm = unit_rows(student_text)
    simg_own = simg_unit.astype(jnp.bfloat16)
    stxt_own = stxt_unit.astype(jnp.bfloat16)
    timg_full = lax.all_gather(teacher_image, "loop", axis=1, tiled=True)
    timg = unit_rows(timg_full)[0].astype(jnp.bfloat16)
    ttxt_full = lax.all_to_all(teacher_text, "loop", split_axis=0, concat_axis=1, tiled=True)
    ttxt_own = unit_rows(ttxt_full)[0].astype(jnp.bfloat16)
    simg = lax.all_gather(simg_own, "loop", axis=0, tiled=True)
    stxt, ttxt = (
        lax.all_gather(stxt_own, "row", axis=0, tiled=True),
        lax.all_gather(ttxt_own, "row", axis=0, tiled=True),
    )
    sscale = student_scale[0]
    tscale = teacher_scale[0]
    slog = sscale * jnp.einsum("re,ce->rc", simg, stxt, preferred_element_type=jnp.float32)
    tlog = tscale * jnp.einsum("re,ce->rc", timg, ttxt, preferred_element_type=jnp.float32)
    smax, tmax = lax.pmax((jnp.max(slog, axis=1), jnp.max(tlog, axis=1)), "loop")
    sexp = jnp.exp(slog - smax[:, None])
    texp = jnp.exp(tlog - tmax[:, None])
    ssum, tsum, cross = lax.psum(
        (jnp.sum(sexp, axis=1), jnp.sum(texp, axis=1), jnp.sum(texp * (tlog - slog), axis=1)),
        "loop",
    )
    lses = smax + jnp.log(ssum)
    lset = tmax + jnp.log(tsum)
    diverge = cross / tsum - lset + lses
    group_total = lax.psum(jnp.sum(diverge), "row")
    batch_total = simg.shape[0] * lax.axis_size("row")
    loss = (group_total / batch_total).reshape(1)
    probs = jnp.exp(slog - lses[:, None])
    probt = jnp.exp(tlog - lset[:, None])
    grad_logits = (sscale * (probs - probt)).astype(jnp.bfloat16)
    dimg = lax.psum_scatter(
        jnp.dot(grad_logits, stxt, preferred_element_type=jnp.float32).astype(jnp.bfloat16),
        "loop",
        scatter_dimension=0,
        tiled=True,
    ).astype(jnp.float32)
    dtxt = lax.psum_scatter(
        jnp.einsum("rc,re->ce", grad_logits, simg, preferred_element_type=jnp.float32).astype(
            jnp.bfloat16
        ),
        "row",
        scatter_dimension=0,
        tiled=True,
    ).astype(jnp.float32)
    return (loss, back_norm(dimg, simg_unit, simg_norm), back_norm(dtxt, stxt_unit, stxt_norm))


def solution(mesh):
    return jax.shard_map(
        on_device,
        mesh=mesh,
        in_specs=(
            P(("row", "loop"), None),
            P(("row", "loop"), None),
            P("row", "loop"),
            P("row", "loop"),
            P(),
            P(),
        ),
        out_specs=(P(), P(("row", "loop"), None), P(("row", "loop"), None)),
        check_vma=False,
    )
```

profile of v0, /device:TPU:0, one launch (start us, length us, event | category | flops | bytes accessed | tf_op | source)
XLA Modules:
  0.0 265.1 jit_solution(4238910627074843657)
XLA Ops:
  7.2 0.0 copy-start.3
  7.2 0.0 all-gather.5.cloned.1.call-start
  7.2 0.7 all-gather.5.cloned.1.call-update
  7.9 0.0 all-gather.9.cloned.1.call-start
  8.0 1.1 fusion.5
  9.1 1.8 fusion.14
  10.9 0.0 all-gather.9.cloned.1.call-update
  10.9 0.0 all-gather.11.cloned.1.call-start
  11.0 1.1 fusion.6
  12.1 1.8 fusion.15
  14.0 0.0 all-gather.11.cloned.1.call-update
  14.0 0.0 all-gather.7.cloned.1.call-start
  14.0 0.0 copy-done.3
  14.0 14.7 %all_to_all.13 = bf16[4,160,256]{2,1,0:T(8,128)(2,1)S(1)} all-to-all(bf16[4,160,256]{2,1,0:T(8,128)(2,1)S(1)} %bitcast.19), channel_id=1, replica_groups=mesh['row'=8,'loop'=4] {'loop'}, dimensions={0} | all-to-all | bytes 655360 | tf_op jit(solution)/shard_map/all_to_all | solution.py:29
  28.8 0.1 copy.11
  28.8 0.1 fusion.13
  29.0 0.9 divide_convert_fusion
  29.9 0.0 all-gather.7.cloned.1.call-update
  29.9 0.0 reduce-scatter.3.cloned.1.call-start
  31.2 12.3 %all-gather.5.cloned.1.call-done = bf16[640,1024]{1,0:T(8,128)(2,1)} async-done(((bf16[640,256]{1,0:T(8,128)(2,1)}), bf16[640,1024]{1,0:T(8,128)(2,1)}) %all-gather.5.cloned.1.call-update) | async-done | bytes 1310736 | tf_op jit(solution)/shard_map/all_gather | solution.py:27
  43.5 1.6 fusion.1
  45.2 29.5 %all-gather.9.cloned.1.call-done = bf16[640,1024]{1,0:T(8,128)(2,1)} async-done(((bf16[160,1024]{1,0:T(8,128)(2,1)}), bf16[640,1024]{1,0:T(8,128)(2,1)}) %all-gather.9.cloned.1.call-update) | async-done | bytes 1310736 | tf_op jit(solution)/shard_map/all_gather | solution.py:31
  74.6 35.4 %all-gather.11.cloned.1.call-done = bf16[1280,1024]{1,0:T(8,128)(2,1)} async-done(((bf16[160,1024]{1,0:T(8,128)(2,1)}), bf16[1280,1024]{1,0:T(8,128)(2,1)}) %all-gather.11.cloned.1.call-update) | async-done | bytes 2621456 | tf_op jit(solution)/shard_map/all_gather | solution.py:33
  110.0 4.2 %fusion.16 = (f32[640]{0:T(1024)S(1)}, f32[640,1280]{1,0:T(8,128)S(1)}) fusion(bf16[640,1024]{1,0:T(8,128)(2,1)} %all-gather.9.cloned.1.call-done, bf16[1280,1024]{1,0:T(8,128)(2,1)} %all-gather.11.cloned.1.call-done, f32[]{:T(128)} %bitcast.15), kind=kOutput, calls=%fused_computation.43 | convolution fusion | flops 1679359360 | bytes 7211524 | tf_op jit(solution)/shard_map/re,ce->rc/dot_general | solution.py:38
  114.2 30.8 %all-gather.7.cloned.1.call-done = bf16[1280,1024]{1,0:T(8,128)(2,1)} async-done(((bf16[160,1024]{1,0:T(8,128)(2,1)}), bf16[1280,1024]{1,0:T(8,128)(2,1)}) %all-gather.7.cloned.1.call-update) | async-done | bytes 2621456 | tf_op jit(solution)/shard_map/all_gather | solution.py:34
  144.9 5.8 %fusion.17 = (f32[640]{0:T(1024)S(1)}, f32[640,1280]{1,0:T(8,128)}) fusion(bf16[1280,1024]{1,0:T(8,128)(2,1)} %all-gather.7.cloned.1.call-done, bf16[640,1024]{1,0:T(8,128)(2,1)} %all-gather.5.cloned.1.call-done, f32[640]{0:T(1024)S(1)} %add_sqrt_fusion, f32[]{:T(128)} %bitcast.17), kind=kOutput, calls=%fused_computation.44 | convolution fusion | flops 1681325440 | bytes 7214084 | tf_op jit(solution)/shard_map/re,ce->rc/dot_general | solution.py:39
  150.7 10.0 %all-reduce.1 = (f32[640]{0:T(1024)S(1)}, f32[640]{0:T(1024)S(1)}) all-reduce(f32[640]{0:T(1024)S(1)} %get-tuple-element.14, f32[640]{0:T(1024)S(1)} %get-tuple-element.16), channel_id=1, replica_groups=mesh['row'=8,'loop'=4] {'loop'}, use_global_device_ids=true, to_apply=%region_11.0 | all-reduce | flops 1280 | bytes 10240 | tf_op jit(solution)/shard_map/pmax | solution.py:40
  160.7 3.3 %multiply_reduce_fusion = (f32[640]{0:T(1024)S(1)}, f32[640]{0:T(1024)S(1)}, f32[640]{0:T(1024)S(1)}) fusion(f32[640,1280]{1,0:T(8,128)} %get-tuple-element.17, f32[640,1280]{1,0:T(8,128)S(1)} %get-tuple-element.15, f32[640]{0:T(1024)S(1)} %get-tuple-element.10, f32[640]{0:T(1024)S(1)} %get-tuple-element.9), kind=kLoop, calls=%fused_computation.5 | loop fusion | flops 5732480 | bytes 6566400 | tf_op jit(solution)/shard_map/reduce_sum | solution.py:44
  164.0 14.0 %all-reduce = (f32[640]{0:T(1024)S(1)}, f32[640]{0:T(1024)S(1)}, f32[640]{0:T(1024)S(1)}) all-reduce(f32[640]{0:T(1024)S(1)} %get-tuple-element.5, f32[640]{0:T(1024)S(1)} %get-tuple-element.4, f32[640]{0:T(1024)S(1)} %get-tuple-element.3), channel_id=1, replica_groups=mesh['row'=8,'loop'=4] {'loop'}, use_global_device_ids=true, to_apply=%region_13.0 | all-reduce | flops 1920 | bytes 15360 | tf_op jit(solution)/shard_map/psum | solution.py:43
  178.1 0.6 add_reduce_fusion
  178.7 3.0 %multiply_convert_fusion = bf16[640,1280]{1,0:T(8,128)(2,1)S(1)} fusion(f32[640,1280]{1,0:T(8,128)} %get-tuple-element.17, f32[640,1280]{1,0:T(8,128)S(1)} %get-tuple-element.15, f32[640]{0:T(1024)S(1)} %get-tuple-element.12, f32[640]{0:T(1024)S(1)} %get-tuple-element.13, f32[]{:T(128)} %bitcast.16), kind=kLoop, calls=%fused_computation.3 | loop fusion | flops 4096000 | bytes 8197124 | tf_op jit(solution)/shard_map/convert_element_type | solution.py:55
  181.7 0.0 copy-start.2
  181.7 1.2 copy-done.2
  182.9 0.0 copy-done.4
  182.9 3.0 %convolution_convert_fusion.1 = bf16[640,1024]{1,0:T(8,128)(2,1)} fusion(bf16[640,1280]{1,0:T(8,128)(2,1)S(1)} %multiply_convert_fusion, bf16[1280,1024]{1,0:T(8,128)(2,1)S(1)} %copy-done.4), kind=kOutput, calls=%fused_computation.12 | convolution fusion | flops 1678376960 | bytes 5570560 | tf_op jit(solution)/shard_map/dot_general | solution.py:57
  185.9 0.0 reduce-scatter.3.cloned.1.call-update
  185.9 0.0 reduce-scatter.5.cloned.1.call-start
  186.0 0.0 copy-done.5
  186.0 5.2 %convolution_convert_fusion = bf16[1280,1024]{1,0:T(8,128)(2,1)} fusion(bf16[640,1280]{1,0:T(8,128)(2,1)} %copy-done.2, bf16[640,1024]{1,0:T(8,128)(2,1)S(1)} %copy-done.5), kind=kOutput, calls=%fused_computation | convolution fusion | flops 1679032320 | bytes 5570560 | tf_op jit(solution)/shard_map/rc,re->ce/dot_general | solution.py:63
  191.2 0.0 reduce-scatter.5.cloned.1.call-update
  191.2 14.2 %psum.31 = f32[]{:T(128)} all-reduce(f32[]{:T(128)} %get-tuple-element.11), channel_id=1, replica_groups=mesh['row'=8,'loop'=4] {'row'}, use_global_device_ids=true, to_apply=%region_15.0 | all-reduce | flops 1 | bytes 8 | tf_op jit(solution)/shard_map/psum | solution.py:50
  206.1 7.7 %reduce-scatter.3.cloned.1.call-done = bf16[160,1024]{1,0:T(8,128)(2,1)} async-done(((bf16[640,1024]{1,0:T(8,128)(2,1)}), bf16[160,1024]{1,0:T(8,128)(2,1)}) %reduce-scatter.3.cloned.1.call-update) | async-done | bytes 327696 | tf_op jit(solution)/shard_map/reduce_scatter | solution.py:56
  213.8 0.0 copy-done
  213.8 1.2 fusion.7
  215.0 2.0 fusion.9
  217.0 37.0 %reduce-scatter.5.cloned.1.call-done = bf16[160,1024]{1,0:T(8,128)(2,1)} async-done(((bf16[1280,1024]{1,0:T(8,128)(2,1)}), bf16[160,1024]{1,0:T(8,128)(2,1)}) %reduce-scatter.5.cloned.1.call-update) | async-done | bytes 327696 | tf_op jit(solution)/shard_map/reduce_scatter | solution.py:62
  253.9 1.2 fusion.10
  255.2 2.0 fusion.12
  (10 shorter events, 0.1 us)
Async XLA Ops:
  7.2 6.9 %copy-start.3 = (bf16[640,256]{1,0:T(8,128)(2,1)S(1)}, bf16[640,256]{1,0:T(8,128)(2,1)}, u32[]{:S(2)}) copy-start(bf16[640,256]{1,0:T(8,128)(2,1)} %param.9) | copy-start | bytes 983044
  7.2 36.3 %all-gather.5.cloned.1.call-start = ((), (), s32[]{:S(2)}) async-start(), calls=%async_computation.3 | async-start | bytes 1638400 | tf_op jit(solution)/shard_map/all_gather | solution.py:27
  7.9 66.7 %all-gather.9.cloned.1.call-start = ((), (), s32[]{:S(2)}) async-start(), calls=%async_computation.5 | async-start | bytes 1638400 | tf_op jit(solution)/shard_map/all_gather | solution.py:31
  10.9 99.1 %all-gather.11.cloned.1.call-start = ((), (), s32[]{:S(2)}) async-start(), calls=%async_computation.6 | async-start | bytes 2949120 | tf_op jit(solution)/shard_map/all_gather | solution.py:33
  14.0 131.0 %all-gather.7.cloned.1.call-start = ((), (), s32[]{:S(2)}) async-start(), calls=%async_computation.4 | async-start | bytes 2949120 | tf_op jit(solution)/shard_map/all_gather | solution.py:34
  29.9 183.9 %reduce-scatter.3.cloned.1.call-start = ((), (), s32[]{:S(2)}) async-start(), calls=%async_computation.7 | async-start | bytes 1638400 | tf_op jit(solution)/shard_map/reduce_scatter | solution.py:56
  178.7 4.2 %copy-start.4 = (bf16[1280,1024]{1,0:T(8,128)(2,1)S(1)}, bf16[1280,1024]{1,0:T(8,128)(2,1)}, u32[]{:S(2)}) copy-start(bf16[1280,1024]{1,0:T(8,128)(2,1)} %all-gather.11.cloned.1.call-done) | copy-start | bytes 7864324
  181.7 1.2 copy-start.2
  182.9 3.1 %copy-start.5 = (bf16[640,1024]{1,0:T(8,128)(2,1)S(1)}, bf16[640,1024]{1,0:T(8,128)(2,1)}, u32[]{:S(2)}) copy-start(bf16[640,1024]{1,0:T(8,128)(2,1)} %all-gather.9.cloned.1.call-done) | copy-start | bytes 3932164
  185.9 68.0 %reduce-scatter.5.cloned.1.call-start = ((), (), s32[]{:S(2)}) async-start(), calls=%async_computation.8 | async-start | bytes 2949120 | tf_op jit(solution)/shard_map/reduce_scatter | solution.py:62
  191.2 22.6 %copy-start = (bf16[160,1024]{1,0:T(8,128)(2,1)S(1)}, bf16[160,1024]{1,0:T(8,128)(2,1)}, u32[]{:S(2)}) copy-start(bf16[160,1024]{1,0:T(8,128)(2,1)} %param.6) | copy-start | bytes 983044
  191.2 62.8 %copy-start.1 = (bf16[160,1024]{1,0:T(8,128)(2,1)S(1)}, bf16[160,1024]{1,0:T(8,128)(2,1)}, u32[]{:S(2)}) copy-start(bf16[160,1024]{1,0:T(8,128)(2,1)} %param.7) | copy-start | bytes 983044
Sparse Core Ops, SparseCore 0:
  9.8 33.6 all-gather.4
  45.9 28.6 all-gather.8
  76.3 33.6 all-gather.10
  112.1 32.8 all-gather.6
  186.0 27.6 reduce-scatter.2
  215.9 37.9 reduce-scatter.4
where the time goes:
time: 266 us; the launch traced here: 265 us
  waiting for transfers between devices  153 us (58%)
  blocking collectives  52.9 us (20%)
  other arithmetic  22 us (8%)
  matrix products  18.1 us (7%)
  between operations  17.3 us (7%)
    reduce_scatter x1, waiting for transfers between devices, on_device(): lax.psum_scatter(jnp.einsum('rc,re->ce', grad_logits, simg, preferred_ele...  37 us
    all_gather x1, waiting for transfers between devices, on_device(): lax.all_gather(stxt_own, 'row', axis=0, tiled=True)  35.4 us
    all_gather x1, waiting for transfers between devices, on_device(): lax.all_gather(ttxt_own, 'row', axis=0, tiled=True)  30.8 us
    all_gather x1, waiting for transfers between devices, on_device(): simg = lax.all_gather(simg_own, 'loop', axis=0, tiled=True)  29.5 us
    all_to_all x1, blocking collectives, on_device(): lax.all_to_all(teacher_text, 'loop', split_axis=0, concat_axis=1, tiled=T...  14.7 us
    psum x1, blocking collectives, on_device(): group_total = lax.psum(jnp.sum(diverge), 'row')  14.2 us
    psum x1, blocking collectives, on_device(): lax.psum((jnp.sum(sexp, axis=1), jnp.sum(texp, axis=1), jnp.sum(texp * (t...  14 us
    all_gather x1, waiting for transfers between devices, on_device(): timg_full = lax.all_gather(teacher_image, 'loop', axis=1, tiled=True)  12.3 us
  transfers between devices with their start and end apart: 6, of which 6 were waited for; matrix products, arithmetic and copies ran while one was open for 8% of the time, Pallas kernels for 0%

commit v1 on v0

--- a/solution.py
+++ b/solution.py
@@ -4,6 +4,13 @@
 from jax.sharding import PartitionSpec as P
 
 EPS = 1e-06
+
+
+def swapped_in(x, axis, dim):
+    size = lax.axis_size(axis)
+    tiles = jnp.stack([x for _ in range(size)])
+    tiles = lax.all_to_all(tiles, axis, split_axis=0, concat_axis=0)
+    return jnp.concatenate(tiles, axis=dim)
 
 
 def unit_rows(codes):
@@ -31,7 +38,7 @@
     simg = lax.all_gather(simg_own, "loop", axis=0, tiled=True)
     stxt, ttxt = (
         lax.all_gather(stxt_own, "row", axis=0, tiled=True),
-        lax.all_gather(ttxt_own, "row", axis=0, tiled=True),
+        swapped_in(ttxt_own, "row", 0),
     )
     sscale = student_scale[0]
     tscale = teacher_scale[0]

time: 266 us -> 236 us (0.89)
  waiting for transfers between devices: 153 us -> 128 us
  blocking collectives: 52.9 us -> 38.2 us
  starting transfers between devices: 0.24 us -> 10.2 us
    all_gather x1 -> x0, waiting for transfers between devices: 30.8 us -> none  [on_device(): lax.all_gather(ttxt_own, 'row', axis=0, tiled=True)]
    all_to_all x1 -> x0, blocking collectives: 14.7 us -> none  [on_device(): lax.all_to_all(teacher_text, 'loop', split_axis=0, concat_axis=1, tiled=T...]
    all_to_all x0 -> x2, starting transfers between devices: none -> 10.1 us  [the longest x1 5.2 us: on_device(): lax.all_to_all(teacher_text, 'loop', split_axis=0, concat_axis=1, tiled=T...]
    all_gather x1, waiting for transfers between devices: 35.4 us -> 39.9 us  [on_device(): lax.all_gather(stxt_own, 'row', axis=0, tiled=True)]
    all_to_all x0 -> x2, waiting for transfers between devices: none -> 3.87 us  [the longest x1 3.86 us: on_device(): lax.all_to_all(teacher_text, 'loop', split_axis=0, concat_axis=1, tiled=T...]
  transfers between devices with their start and end apart: 6 -> 7, of which waited for: 6 -> 6; matrix products, arithmetic and copies ran while one was open for 8% -> 9% of each run, Pallas kernels for 0% -> 0%
where the time goes in v1:
time: 236 us; the launch traced here: 235 us
  waiting for transfers between devices  128 us (54%)
  blocking collectives  38.2 us (16%)
  other arithmetic  20.3 us (9%)
  matrix products  18.1 us (8%)
  between operations  17 us (7%)
  starting transfers between devices  10.2 us (4%)
  local copies, waits for them, and re-layouts  3.11 us (1%)
    all_gather x1, waiting for transfers between devices, on_device(): lax.all_gather(stxt_own, 'row', axis=0, tiled=True)  39.9 us
    reduce_scatter x1, waiting for transfers between devices, on_device(): lax.psum_scatter(jnp.einsum('rc,re->ce', grad_logits, simg, preferred_ele...  36.8 us
    all_gather x1, waiting for transfers between devices, on_device(): simg = lax.all_gather(simg_own, 'loop', axis=0, tiled=True)  29.5 us
    psum x1, blocking collectives, on_device(): lax.psum((jnp.sum(sexp, axis=1), jnp.sum(texp, axis=1), jnp.sum(texp * (t...  14.9 us
    psum x1, blocking collectives, on_device(): group_total = lax.psum(jnp.sum(diverge), 'row')  14.2 us
    all_gather x1, waiting for transfers between devices, on_device(): timg_full = lax.all_gather(teacher_image, 'loop', axis=1, tiled=True)  10.6 us
    pmax x1, blocking collectives, on_device(): lax.pmax((jnp.max(slog, axis=1), jnp.max(tlog, axis=1)), 'loop')  9.03 us
    reduce_scatter x1, waiting for transfers between devices, on_device(): lax.psum_scatter(jnp.dot(grad_logits, stxt, preferred_element_type=jnp.fl...  6.64 us
  transfers between devices with their start and end apart: 7, of which 6 were waited for; matrix products, arithmetic and copies ran while one was open for 9% of the time, Pallas kernels for 0%

profile of v1, /device:TPU:0, one launch (start us, length us, event | category | flops | bytes accessed | tf_op | source)
XLA Modules:
  0.0 234.9 jit_solution(9843186742077251693)
XLA Ops:
  7.2 0.0 copy-start.1
  7.2 0.0 all-gather.4.cloned.1.call-start
  7.2 0.7 all-gather.4.cloned.1.call-update
  7.9 0.0 all-gather.6.cloned.1.call-start
  8.0 1.1 fusion.5
  9.1 1.8 fusion.14
  10.9 0.0 all-gather.6.cloned.1.call-update
  10.9 5.2 %all-to-all-start = ((bf16[4,160,256]{2,1,0:T(8,128)(2,1)}), bf16[4,160,256]{2,1,0:T(8,128)(2,1)S(1)}, u32[]{:S(2)}, u32[]{:S(2)}) async-start(bf16[4,160,256]{2,1,0:T(8,128)(2,1)} %bitcast.20), calls=%async_computation | async-start | bytes 655360 | tf_op jit(solution)/shard_map/all_to_all | solution.py:36
  16.2 0.0 all-gather.8.cloned.1.call-start
  16.2 1.1 fusion.6
  17.3 0.0 copy-done.1
  17.3 0.9 fusion.15
  18.2 0.0 all-gather.8.cloned.1.call-update
  18.2 3.9 %all-to-all-done = bf16[4,160,256]{2,1,0:T(8,128)(2,1)S(1)} async-done(((bf16[4,160,256]{2,1,0:T(8,128)(2,1)}), bf16[4,160,256]{2,1,0:T(8,128)(2,1)S(1)}, u32[]{:S(2)}, u32[]{:S(2)}) %all-to-all-start) | async-done | bytes 327712 | tf_op jit(solution)/shard_map/all_to_all | solution.py:36
  22.1 0.1 fusion.13
  22.2 0.1 copy.11
  22.3 0.1 divide_convert_fusion
  22.5 1.8 stack.2
  24.3 4.9 %all-to-all-start.1 = ((bf16[8,160,1024]{2,1,0:T(8,128)(2,1)}), bf16[8,160,1024]{2,1,0:T(8,128)(2,1)}, u32[]{:S(2)}, u32[]{:S(2)}) async-start(bf16[8,160,1024]{2,1,0:T(8,128)(2,1)} %stack.2), calls=%async_computation.1 | async-start | bytes 5242880 | tf_op jit(solution)/shard_map/all_to_all | solution.py:12
  29.2 0.0 reduce-scatter.3.cloned.1.call-start
  30.5 10.6 %all-gather.4.cloned.1.call-done = bf16[640,1024]{1,0:T(8,128)(2,1)} async-done(((bf16[640,256]{1,0:T(8,128)(2,1)}), bf16[640,1024]{1,0:T(8,128)(2,1)}) %all-gather.4.cloned.1.call-update) | async-done | bytes 1310736 | tf_op jit(solution)/shard_map/all_gather | solution.py:34
  41.1 1.6 fusion.1
  42.8 29.5 %all-gather.6.cloned.1.call-done = bf16[640,1024]{1,0:T(8,128)(2,1)} async-done(((bf16[160,1024]{1,0:T(8,128)(2,1)}), bf16[640,1024]{1,0:T(8,128)(2,1)}) %all-gather.6.cloned.1.call-update) | async-done | bytes 1310736 | tf_op jit(solution)/shard_map/all_gather | solution.py:38
  72.2 39.9 %all-gather.8.cloned.1.call-done = bf16[1280,1024]{1,0:T(8,128)(2,1)} async-done(((bf16[160,1024]{1,0:T(8,128)(2,1)}), bf16[1280,1024]{1,0:T(8,128)(2,1)}) %all-gather.8.cloned.1.call-update) | async-done | bytes 2621456 | tf_op jit(solution)/shard_map/all_gather | solution.py:40
  112.1 4.2 %fusion.16 = (f32[640]{0:T(1024)S(1)}, f32[640,1280]{1,0:T(8,128)S(1)}) fusion(bf16[640,1024]{1,0:T(8,128)(2,1)} %all-gather.6.cloned.1.call-done, bf16[1280,1024]{1,0:T(8,128)(2,1)} %all-gather.8.cloned.1.call-done, f32[]{:T(128)} %bitcast.16), kind=kOutput, calls=%fused_computation.43 | convolution fusion | flops 1679359360 | bytes 7211524 | tf_op jit(solution)/shard_map/re,ce->rc/dot_general | solution.py:45
  116.3 0.0 all-to-all-done.1
  116.3 5.8 %fusion.17 = (f32[640]{0:T(1024)S(1)}, f32[640,1280]{1,0:T(8,128)}) fusion(bf16[1280,1024]{1,0:T(8,128)(2,1)} %bitcast.3, bf16[640,1024]{1,0:T(8,128)(2,1)} %all-gather.4.cloned.1.call-done, f32[640]{0:T(1024)S(1)} %add_sqrt_fusion, f32[]{:T(128)} %bitcast.18), kind=kOutput, calls=%fused_computation.44 | convolution fusion | flops 1681325440 | bytes 7214084 | tf_op jit(solution)/shard_map/re,ce->rc/dot_general | solution.py:46
  122.1 9.0 %all-reduce.1 = (f32[640]{0:T(1024)S(1)}, f32[640]{0:T(1024)S(1)}) all-reduce(f32[640]{0:T(1024)S(1)} %get-tuple-element.14, f32[640]{0:T(1024)S(1)} %get-tuple-element.16), channel_id=1, replica_groups=mesh['row'=8,'loop'=4] {'loop'}, use_global_device_ids=true, to_apply=%region_11.0 | all-reduce | flops 1280 | bytes 10240 | tf_op jit(solution)/shard_map/pmax | solution.py:47
  131.1 3.3 %multiply_reduce_fusion = (f32[640]{0:T(1024)S(1)}, f32[640]{0:T(1024)S(1)}, f32[640]{0:T(1024)S(1)}) fusion(f32[640,1280]{1,0:T(8,128)} %get-tuple-element.17, f32[640,1280]{1,0:T(8,128)S(1)} %get-tuple-element.15, f32[640]{0:T(1024)S(1)} %get-tuple-element.10, f32[640]{0:T(1024)S(1)} %get-tuple-element.9), kind=kLoop, calls=%fused_computation.5 | loop fusion | flops 5732480 | bytes 6566400 | tf_op jit(solution)/shard_map/reduce_sum | solution.py:51
  134.4 14.9 %all-reduce = (f32[640]{0:T(1024)S(1)}, f32[640]{0:T(1024)S(1)}, f32[640]{0:T(1024)S(1)}) all-reduce(f32[640]{0:T(1024)S(1)} %get-tuple-element.5, f32[640]{0:T(1024)S(1)} %get-tuple-element.4, f32[640]{0:T(1024)S(1)} %get-tuple-element.3), channel_id=1, replica_groups=mesh['row'=8,'loop'=4] {'loop'}, use_global_device_ids=true, to_apply=%region_13.0 | all-reduce | flops 1920 | bytes 15360 | tf_op jit(solution)/shard_map/psum | solution.py:50
  149.4 0.6 add_reduce_fusion
  150.0 3.0 %multiply_convert_fusion = bf16[640,1280]{1,0:T(8,128)(2,1)S(1)} fusion(f32[640,1280]{1,0:T(8,128)} %get-tuple-element.17, f32[640,1280]{1,0:T(8,128)S(1)} %get-tuple-element.15, f32[640]{0:T(1024)S(1)} %get-tuple-element.12, f32[640]{0:T(1024)S(1)} %get-tuple-element.13, f32[]{:T(128)} %bitcast.17), kind=kLoop, calls=%fused_computation.3 | loop fusion | flops 4096000 | bytes 8197124 | tf_op jit(solution)/shard_map/convert_element_type | solution.py:62
  153.0 0.0 copy-start.3
  153.0 1.2 copy-done.3
  154.2 0.0 copy-done.4
  154.2 3.0 %convolution_convert_fusion.1 = bf16[640,1024]{1,0:T(8,128)(2,1)} fusion(bf16[640,1280]{1,0:T(8,128)(2,1)S(1)} %multiply_convert_fusion, bf16[1280,1024]{1,0:T(8,128)(2,1)S(1)} %copy-done.4), kind=kOutput, calls=%fused_computation.12 | convolution fusion | flops 1678376960 | bytes 5570560 | tf_op jit(solution)/shard_map/dot_general | solution.py:64
  157.2 0.0 reduce-scatter.3.cloned.1.call-update
  157.2 0.0 reduce-scatter.5.cloned.1.call-start
  157.3 5.2 %convolution_convert_fusion = bf16[1280,1024]{1,0:T(8,128)(2,1)} fusion(bf16[640,1280]{1,0:T(8,128)(2,1)} %copy-done.3, bf16[640,1024]{1,0:T(8,128)(2,1)S(1)} %copy-done.5), kind=kOutput, calls=%fused_computation | convolution fusion | flops 1679032320 | bytes 5570560 | tf_op jit(solution)/shard_map/rc,re->ce/dot_general | solution.py:70
  162.5 0.0 reduce-scatter.5.cloned.1.call-update
  162.5 14.2 %psum.31 = f32[]{:T(128)} all-reduce(f32[]{:T(128)} %get-tuple-element.11), channel_id=1, replica_groups=mesh['row'=8,'loop'=4] {'row'}, use_global_device_ids=true, to_apply=%region_15.0 | all-reduce | flops 1 | bytes 8 | tf_op jit(solution)/shard_map/psum | solution.py:57
  177.4 6.6 %reduce-scatter.3.cloned.1.call-done = bf16[160,1024]{1,0:T(8,128)(2,1)} async-done(((bf16[640,1024]{1,0:T(8,128)(2,1)}), bf16[160,1024]{1,0:T(8,128)(2,1)}) %reduce-scatter.3.cloned.1.call-update) | async-done | bytes 327696 | tf_op jit(solution)/shard_map/reduce_scatter | solution.py:63
  184.0 1.2 fusion.7
  185.3 2.0 fusion.9
  187.2 36.8 %reduce-scatter.5.cloned.1.call-done = bf16[160,1024]{1,0:T(8,128)(2,1)} async-done(((bf16[1280,1024]{1,0:T(8,128)(2,1)}), bf16[160,1024]{1,0:T(8,128)(2,1)}) %reduce-scatter.5.cloned.1.call-update) | async-done | bytes 327696 | tf_op jit(solution)/shard_map/reduce_scatter | solution.py:69
  224.0 0.0 copy-done.2
  224.0 1.2 fusion.10
  225.3 2.0 fusion.12
  (11 shorter events, 0.1 us)
Async XLA Ops:
  7.2 10.1 %copy-start.1 = (bf16[160,1024]{1,0:T(8,128)(2,1)S(1)}, bf16[160,1024]{1,0:T(8,128)(2,1)}, u32[]{:S(2)}) copy-start(bf16[160,1024]{1,0:T(8,128)(2,1)} %param.7) | copy-start | bytes 983044
  7.2 33.9 %all-gather.4.cloned.1.call-start = ((), (), s32[]{:S(2)}) async-start(), calls=%async_computation.4 | async-start | bytes 1638400 | tf_op jit(solution)/shard_map/all_gather | solution.py:34
  7.9 64.3 %all-gather.6.cloned.1.call-start = ((), (), s32[]{:S(2)}) async-start(), calls=%async_computation.5 | async-start | bytes 1638400 | tf_op jit(solution)/shard_map/all_gather | solution.py:38
  10.9 11.1 %all-to-all-start = ((bf16[4,160,256]{2,1,0:T(8,128)(2,1)}), bf16[4,160,256]{2,1,0:T(8,128)(2,1)S(1)}, u32[]{:S(2)}, u32[]{:S(2)}) async-start(bf16[4,160,256]{2,1,0:T(8,128)(2,1)} %bitcast.20), calls=%async_computation | async-start | bytes 655360 | tf_op jit(solution)/shard_map/all_to_all | solution.py:36
  16.2 96.0 %all-gather.8.cloned.1.call-start = ((), (), s32[]{:S(2)}) async-start(), calls=%async_computation.6 | async-start | bytes 2949120 | tf_op jit(solution)/shard_map/all_gather | solution.py:40
  24.3 92.0 %all-to-all-start.1 = ((bf16[8,160,1024]{2,1,0:T(8,128)(2,1)}), bf16[8,160,1024]{2,1,0:T(8,128)(2,1)}, u32[]{:S(2)}, u32[]{:S(2)}) async-start(bf16[8,160,1024]{2,1,0:T(8,128)(2,1)} %stack.2), calls=%async_computation.1 | async-start | bytes 5242880 | tf_op jit(solution)/shard_map/all_to_all | solution.py:12
  29.2 154.9 %reduce-scatter.3.cloned.1.call-start = ((), (), s32[]{:S(2)}) async-start(), calls=%async_computation.7 | async-start | bytes 1638400 | tf_op jit(solution)/shard_map/reduce_scatter | solution.py:63
  150.0 4.2 %copy-start.4 = (bf16[1280,1024]{1,0:T(8,128)(2,1)S(1)}, bf16[1280,1024]{1,0:T(8,128)(2,1)}, u32[]{:S(2)}) copy-start(bf16[1280,1024]{1,0:T(8,128)(2,1)} %all-gather.8.cloned.1.call-done) | copy-start | bytes 7864324
  153.0 1.2 copy-start.3
  154.2 3.1 %copy-start.5 = (bf16[640,1024]{1,0:T(8,128)(2,1)S(1)}, bf16[640,1024]{1,0:T(8,128)(2,1)}, u32[]{:S(2)}) copy-start(bf16[640,1024]{1,0:T(8,128)(2,1)} %all-gather.6.cloned.1.call-done) | copy-start | bytes 3932164
  157.2 66.8 %reduce-scatter.5.cloned.1.call-start = ((), (), s32[]{:S(2)}) async-start(), calls=%async_computation.8 | async-start | bytes 2949120 | tf_op jit(solution)/shard_map/reduce_scatter | solution.py:69
  162.5 21.6 %copy-start = (bf16[160,1024]{1,0:T(8,128)(2,1)S(1)}, bf16[160,1024]{1,0:T(8,128)(2,1)}, u32[]{:S(2)}) copy-start(bf16[160,1024]{1,0:T(8,128)(2,1)} %param.6) | copy-start | bytes 983044
  162.5 61.6 %copy-start.2 = (bf16[160,1024]{1,0:T(8,128)(2,1)S(1)}, bf16[160,1024]{1,0:T(8,128)(2,1)}, u32[]{:S(2)}) copy-start(bf16[160,1024]{1,0:T(8,128)(2,1)} %param.7) | copy-start | bytes 983044
Sparse Core Ops, SparseCore 0:
  9.8 31.2 all-gather.3
  43.5 28.6 all-gather.5
  74.4 37.6 all-gather.7
  157.3 26.6 reduce-scatter.2
  186.2 37.8 reduce-scatter.4
